TPU v7x, 512 devices: a whole 4x4x16 slice. The times are simulated.
512 devices in a mesh: dp: 8 (over x, z_hi), tp: 16 (over z_lo, core), sec: 4 (over y).
Axes of the slice: x: 4, y: 4, z: 16 (z_hi: 2, z_lo: 8; z = z_hi * 8 + z_lo), core: 2. Of those that a mesh axis runs over, the one named last changes fastest.
Arguments:
- hidden_states: bfloat16 [4, 512, 8192], P(None, ('dp', 'sec')), may hold values from -6 to 6
- w_query: bfloat16 [8192, 8192], P(('dp', 'sec'), 'tp'), may hold values from -0.0625 to 0.0625
- w_keyval: bfloat16 [8192, 2048], P(('dp', 'sec'), 'tp'), may hold values from -0.0625 to 0.0625
- key_cache: bfloat16 [512, 16, 256, 128], P(('dp', 'sec'), 'tp'), may hold values from -200 to 200, as said below
- value_cache: bfloat16 [512, 16, 256, 128], P(('dp', 'sec'), 'tp'), may hold values from -6 to 6
- cache_begin: int32 [512], P(('dp', 'sec')), may hold values from 0 to 128
- cache_end: int32 [512], P(('dp', 'sec')), may hold values from 256 to 512
Outputs:
- handoff: bfloat16 [4, 512, 8192], P(None, 'dp', ('tp', 'sec'))
Inputs may be any that keep to these rules, and one draw needn't show every extreme that they name: `key_cache`: cached keys; largest magnitudes differ between draws.
All inputs are finite; a program needn't handle non-finite values.
Results may differ from a plain program's by a relative error of at most 0.04.
Values may be sent and summed in bfloat16 or wider, within the bound.
No kernel may reach another device: no remote copies, remote signals or barrier semaphores. Data moves between devices by JAX's collectives and lax.ppermute only.
A program may use at most 64 MiB of HBM per device.

v0:
```python
import jax
import jax.numpy as jnp
from jax import lax
from jax.sharding import PartitionSpec as P

THETA = 500000.0


def in_one_piece(arrays, axis, dim, along):
    both = jnp.concatenate(arrays, axis=along)
    whole, at, done = (lax.all_gather(both, axis, axis=dim, tiled=True), 0, [])
    for a in arrays:
        done.append(lax.slice_in_dim(whole, at, at + a.shape[along], axis=along))
        at += a.shape[along]
    return tuple(done)


def in_blocks(x, dim, length):
    before, after = (x.shape[:dim], x.shape[dim + 1 :])
    return jnp.moveaxis(x.reshape(*before, length, -1, *after), dim, 0)


def sum_at_owner(x, axis, dim):
    length = lax.axis_size(axis)
    parts = lax.all_to_all(in_blocks(x, dim, length), axis, 0, 0, tiled=True)
    return jnp.sum(parts, axis=0)


def in_one_piece_2(arrays, axis, dim, along):
    ends, at = ([], 0)
    for a in arrays[:-1]:
        at += a.shape[along]
        ends.append(at)
    both = jnp.concatenate(arrays, axis=along)
    return tuple(jnp.split(sum_at_owner(both, axis, dim), ends, axis=along))


def swapped(value, axis, stride):
    mask = 2**stride
    pairs = [(source, source ^ mask) for source in range(lax.axis_size(axis))]
    return lax.ppermute(value, axis, pairs)


def rotate(vector, positions):
    half = vector.shape[-1] // 2
    freq = THETA ** (-(jnp.arange(half, dtype=jnp.float32) * 2.0 / vector.shape[-1]))
    angle = positions[..., None] * freq
    angle = angle.reshape(positions.shape + (1,) * (vector.ndim - positions.ndim - 1) + (half,))
    cosine = jnp.cos(angle)
    sine = jnp.sin(angle)
    first = vector[..., :half]
    second = vector[..., half:]
    return jnp.concatenate(
        [first * cosine - second * sine, second * cosine + first * sine], axis=-1
    )


def make_accumulate(token_rows, pieces):
    return (
        jnp.dot(token_rows, pieces[0], preferred_element_type=jnp.float32),
        jnp.dot(token_rows, pieces[1], preferred_element_type=jnp.float32),
    )


def partial_attention(query, keys, values, live, score_scale):
    scores = (
        jnp.einsum("sbkgd,bkpd->sbkgp", query, keys, preferred_element_type=jnp.float32)
        * score_scale
    )
    live = jnp.broadcast_to(live, scores.shape)
    masked = jnp.where(live, scores, jnp.float32(-1e30))
    maxima = jnp.max(masked, axis=-1)
    expo = jnp.where(live, jnp.exp(masked - maxima[..., None]), jnp.float32(0.0))
    totals = jnp.sum(expo, axis=-1)
    weighted = jnp.einsum(
        "sbkgp,bkpd->sbkgd", expo.astype(jnp.bfloat16), values, preferred_element_type=jnp.float32
    )
    return (maxima, totals, weighted)


def merge_parts(parts):
    overall = parts[0][0]
    for entry in parts[1:]:
        overall = jnp.maximum(overall, entry[0])
    weighted = jnp.zeros_like(parts[0][2])
    totals = jnp.zeros_like(parts[0][1])
    for entry in parts:
        factor = jnp.exp(entry[0] - overall)
        weighted = weighted + entry[2] * factor[..., None]
        totals = totals + entry[1] * factor
    return weighted / totals[..., None]


def body(hidden_states, w_query, w_keyval, key_cache, value_cache, cache_begin, cache_end):
    num_steps, batch_rows, width = hidden_states.shape
    head_size = key_cache.shape[-1]
    query_cols = w_query.shape[1]
    keyval_cols = w_keyval.shape[1]
    local_heads = query_cols // head_size
    half_len = key_cache.shape[2]
    score_scale = head_size ** (-0.5)
    sec_count = lax.axis_size("sec")
    sec_index = lax.axis_index("sec")
    sec_group = lax.all_gather(hidden_states, "sec", axis=1, tiled=True)
    shard_rows = w_query.shape[0]
    dp_count = width // (sec_count * shard_rows)
    group_rows = num_steps * batch_rows * sec_count
    grouped = sec_group.reshape(group_rows, dp_count, sec_count, shard_rows)
    chosen = lax.dynamic_slice_in_dim(grouped, sec_index, 1, 2).reshape(
        group_rows, dp_count * shard_rows
    )
    query_all, keyval_all = make_accumulate(chosen, in_one_piece((w_query, w_keyval), "dp", 0, 1))
    query_acc, keyval_acc = in_one_piece_2(
        (
            query_all.reshape(num_steps, sec_count * batch_rows, query_cols),
            keyval_all.reshape(num_steps, sec_count * batch_rows, keyval_cols),
        ),
        "sec",
        1,
        2,
    )
    query_acc = query_acc.reshape(num_steps * batch_rows, query_cols)
    keyval_acc = keyval_acc.reshape(num_steps * batch_rows, keyval_cols)
    positions = (
        cache_end.astype(jnp.float32)[None, :] + jnp.arange(num_steps, dtype=jnp.float32)[:, None]
    )
    query = rotate(
        query_acc.reshape(num_steps, batch_rows, local_heads, head_size), positions
    ).astype(jnp.bfloat16)
    step_ids = jnp.arange(num_steps, dtype=jnp.int32)
    causal = step_ids[None, :] <= step_ids[:, None]
    parity = lax.axis_index("tp") % 2
    own_proj = keyval_acc.reshape(num_steps, batch_rows, head_size)
    own_proj = jnp.where(parity == 0, rotate(own_proj, positions), own_proj).astype(jnp.bfloat16)
    partner_query, partner_proj = swapped((query, own_proj), "tp", 0)
    new_keys = jnp.where(parity == 0, own_proj, partner_proj)
    new_values = jnp.where(parity == 0, partner_proj, own_proj)
    lower_heads = jnp.where(parity == 0, query, partner_query)
    upper_heads = jnp.where(parity == 0, partner_query, query)
    both_heads = jnp.concatenate([lower_heads, upper_heads], axis=2)[:, :, None]
    cache_pos = parity * half_len + jnp.arange(half_len, dtype=jnp.int32)
    cache_live = (cache_pos[None, :] >= cache_begin[:, None]) & (
        cache_pos[None, :] < cache_end[:, None]
    )
    cache_part = partial_attention(
        both_heads, key_cache, value_cache, cache_live[None, :, None, None, :], score_scale
    )
    mine_start = parity * local_heads
    theirs_start = (1 - parity) * local_heads

    def select_heads(array, start):
        return lax.dynamic_slice_in_dim(array, start, local_heads, 3)

    returned = (
        swapped(select_heads(cache_part[0], theirs_start).astype(jnp.bfloat16), "tp", 0).astype(
            jnp.float32
        ),
        swapped(select_heads(cache_part[1], theirs_start).astype(jnp.bfloat16), "tp", 0).astype(
            jnp.float32
        ),
        swapped(select_heads(cache_part[2], theirs_start).astype(jnp.bfloat16), "tp", 0).astype(
            jnp.float32
        ),
    )
    own_part = (
        select_heads(cache_part[0], mine_start),
        select_heads(cache_part[1], mine_start),
        select_heads(cache_part[2], mine_start),
    )
    fresh_part = partial_attention(
        query[:, :, None],
        jnp.transpose(new_keys, (1, 0, 2))[:, None],
        jnp.transpose(new_values, (1, 0, 2))[:, None],
        causal[:, None, None, None, :],
        score_scale,
    )
    parts = [own_part, returned, fresh_part]
    attended = (
        merge_parts(parts)
        .astype(jnp.bfloat16)
        .reshape(num_steps, batch_rows, local_heads * head_size)
    )
    return lax.all_to_all(attended, "sec", split_axis=2, concat_axis=1, tiled=True)


def solution(mesh):
    return jax.shard_map(
        body,
        mesh=mesh,
        in_specs=(
            P(None, ("dp", "sec"), None),
            P(("dp", "sec"), "tp"),
            P(("dp", "sec"), "tp"),
            P(("dp", "sec"), "tp", None, None),
            P(("dp", "sec"), "tp", None, None),
            P(("dp", "sec")),
            P(("dp", "sec")),
        ),
        out_specs=P(None, "dp", ("tp", "sec")),
        check_vma=False,
    )
```

profile of v0, /device:TPU:96, one launch (start us, length us, event | category | flops | bytes accessed | tf_op | source)
XLA Modules:
  0.0 256.3 jit_solution(2915959011371788293)
XLA Ops:
  6.5 0.7 all-gather.3.cloned.1.call-update
  7.3 1.8 pad_maximum_fusion.1
  9.1 0.7 convert_element_type.51
  9.8 59.0 %all-gather.3.cloned.1.call-done = bf16[4,64,8192]{2,1,0:T(8,128)(2,1)} async-done(((bf16[4,16,8192]{2,1,0:T(8,128)(2,1)}), bf16[4,64,8192]{2,1,0:T(8,128)(2,1)}) %all-gather.3.cloned.1.call-update) | async-done | bytes 4194320 | tf_op jit(solution)/shard_map/all_gather | solution.py:104
  68.7 7.9 %reshape.186 = bf16[256,8,4,256]{3,2,1,0:T(4,128)(2,1)} reshape(bf16[4,64,8192]{2,1,0:T(8,128)(2,1)} %all-gather.3.cloned.1.call-done) | data formatting | bytes 8388608 | tf_op jit(solution)/shard_map/reshape | solution.py:108
  76.6 8.4 %dynamic-slice_reduce_fusion = bf16[256,8,256]{2,1,0:T(8,128)(2,1)S(1)} fusion(bf16[256,8,4,256]{3,2,1,0:T(4,128)(2,1)} %reshape.186, s32[]{:T(128)S(6)} %select_n.69), kind=kLoop, calls=%fused_computation.2 | loop fusion | bytes 2097156 | tf_op jit(solution)/shard_map/dynamic_slice | solution.py:109
  85.0 0.5 dot_general.22
  85.5 118.9 %all-gather.5.cloned.1.call-done = bf16[2048,640]{1,0:T(8,128)(2,1)} async-done(((bf16[256,640]{1,0:T(8,128)(2,1)}), bf16[2048,640]{1,0:T(8,128)(2,1)}) %all-gather.5.cloned.1.call-update) | async-done | bytes 2621456 | tf_op jit(solution)/shard_map/all_gather | solution.py:11
  204.5 1.5 fusion.10
  205.9 2.3 fusion
  208.3 0.9 copy.63
  209.2 4.3 %all-to-all-start = ((f32[4,4,16,640]{3,2,1,0:T(8,128)}), f32[4,4,16,640]{3,2,1,0:T(8,128)S(1)}, u32[]{:S(2)}, u32[]{:S(2)}) async-start(f32[4,4,16,640]{3,2,1,0:T(8,128)} %bitcast.151), calls=%async_computation | async-start | bytes 1310720 | tf_op jit(solution)/shard_map/all_to_all | solution.py:25
  213.9 9.9 %all-to-all-done = f32[4,4,16,640]{3,2,1,0:T(8,128)S(1)} async-done(((f32[4,4,16,640]{3,2,1,0:T(8,128)}), f32[4,4,16,640]{3,2,1,0:T(8,128)S(1)}, u32[]{:S(2)}, u32[]{:S(2)}) %all-to-all-start) | async-done | bytes 655392 | tf_op jit(solution)/shard_map/all_to_all | solution.py:25
  224.3 1.9 collective-permute-start.2
  226.4 2.4 collective-permute-start
  228.9 0.7 fusion.55
  229.9 0.5 fusion.54
  231.2 2.2 collective-permute-start.1
  233.5 2.1 collective-permute-start.4
  235.7 2.2 collective-permute-start.3
  238.0 0.8 collective-permute-done.3
  239.7 0.5 reshape.203
  240.2 8.0 %all_to_all.23 = bf16[4,2,4096]{2,1,0:T(2,128)(2,1)S(1)} all-to-all(bf16[4,2,4096]{2,1,0:T(2,128)(2,1)S(1)} %reshape.203), channel_id=1, replica_groups=mesh['dp'=8,'tp'=16,'sec'=4] {'sec'}, dimensions={0} | all-to-all | bytes 131072 | tf_op jit(solution)/shard_map/all_to_all | solution.py:183
  248.6 0.9 copy.32
  (44 shorter events, 3.6 us)
Async XLA Ops:
  6.5 223.4 %copy-start = (bf16[16,1,256,128]{3,2,1,0:T(8,128)(2,1)S(1)}, bf16[16,1,256,128]{3,2,1,0:T(8,128)(2,1)}, u32[]{:S(2)}) copy-start(bf16[16,1,256,128]{3,2,1,0:T(8,128)(2,1)} %param.10) | copy-start | bytes 3145732
  6.5 62.2 %all-gather.3.cloned.1.call-start = ((), (), s32[]{:S(2)}) async-start(), calls=%async_computation.2 | async-start | bytes 5242880 | tf_op jit(solution)/shard_map/all_gather | solution.py:104
  7.3 197.2 %all-gather.5.cloned.1.call-start = ((), (), s32[]{:S(2)}) async-start(), calls=%async_computation.3 | async-start | bytes 2949120 | tf_op jit(solution)/shard_map/all_gather | solution.py:11
  208.2 5.6 %copy-start.2 = (s32[16]{0:T(128)S(1)}, s32[16]{0:T(128)}, u32[]{:S(2)}) copy-start(s32[16]{0:T(128)} %param.13) | copy-start | bytes 196
  208.2 5.6 %copy-start.3 = (s32[16]{0:T(128)S(1)}, s32[16]{0:T(128)}, u32[]{:S(2)}) copy-start(s32[16]{0:T(128)} %param.12) | copy-start | bytes 196
  209.2 14.6 %all-to-all-start = ((f32[4,4,16,640]{3,2,1,0:T(8,128)}), f32[4,4,16,640]{3,2,1,0:T(8,128)S(1)}, u32[]{:S(2)}, u32[]{:S(2)}) async-start(f32[4,4,16,640]{3,2,1,0:T(8,128)} %bitcast.151), calls=%async_computation | async-start | bytes 1310720 | tf_op jit(solution)/shard_map/all_to_all | solution.py:25
  223.8 7.0 %copy-start.1 = (bf16[16,1,256,128]{3,2,1,0:T(8,128)(2,1)S(1)}, bf16[16,1,256,128]{3,2,1,0:T(8,128)(2,1)}, u32[]{:S(2)}) copy-start(bf16[16,1,256,128]{3,2,1,0:T(8,128)(2,1)} %param.11) | copy-start | bytes 3145732
  224.3 4.5 %collective-permute-start.2 = (bf16[4,16,128]{2,1,0:T(8,128)(2,1)S(1)}, bf16[4,16,128]{2,1,0:T(8,128)(2,1)S(1)}, u32[]{:S(2)}, u32[]{:S(2)}) collective-permute-start(bf16[4,16,128]{2,1,0:T(8,128)(2,1)S(1)} %fusion.37), channel_id=1, source_target_pairs={{0,4},{4,0},{8,12},{12,8},{16,20},{20,16},{24,28},{28,24},{32,36},... | collective-permute-start | bytes 49160 | tf_op jit(solution)/shard_map/ppermute | solution.py:41
  226.4 3.3 %collective-permute-start = (bf16[4,16,4,128]{3,2,0,1:T(4,128)(2,1)S(1)}, bf16[4,16,4,128]{3,2,0,1:T(4,128)(2,1)S(1)}, u32[]{:S(2)}, u32[]{:S(2)}) collective-permute-start(bf16[4,16,4,128]{3,2,0,1:T(4,128)(2,1)S(1)} %pad_maximum_fusion.2), channel_id=1, source_target_pairs={{0,4},{4,0},{8,12},{12,8},{16,20},{20,16},{24,28},{28,24},{32,36},... | collective-permute-start | bytes 196616 | tf_op jit(solution)/shard_map/ppermute | solution.py:41
  231.2 6.7 %collective-permute-start.1 = (bf16[4,16,1,4]{3,0,1,2:T(4,128)(2,1)S(1)}, bf16[4,16,1,4]{3,0,1,2:T(4,128)(2,1)S(1)}, u32[]{:S(2)}, u32[]{:S(2)}) collective-permute-start(bf16[4,16,1,4]{3,0,1,2:T(4,128)(2,1)S(1)} %fusion.44), channel_id=1, source_target_pairs={{0,4},{4,0},{8,12},{12,8},{16,20},{20,16},{24,28},{28,24},{32,36},... | collective-permute-start | bytes 1544 | tf_op jit(solution)/shard_map/ppermute | solution.py:41
  233.5 4.4 %collective-permute-start.4 = (bf16[4,16,1,4]{3,0,1,2:T(4,128)(2,1)S(1)}, bf16[4,16,1,4]{3,0,1,2:T(4,128)(2,1)S(1)}, u32[]{:S(2)}, u32[]{:S(2)}) collective-permute-start(bf16[4,16,1,4]{3,0,1,2:T(4,128)(2,1)S(1)} %fusion.45), channel_id=1, source_target_pairs={{0,4},{4,0},{8,12},{12,8},{16,20},{20,16},{24,28},{28,24},{32,36},... | collective-permute-start | bytes 1544 | tf_op jit(solution)/shard_map/ppermute | solution.py:41
  235.7 3.1 %collective-permute-start.3 = (bf16[4,16,1,4,128]{4,3,0,1,2:T(4,128)(2,1)S(1)}, bf16[4,16,1,4,128]{4,3,0,1,2:T(4,128)(2,1)S(1)}, u32[]{:S(2)}, u32[]{:S(2)}) collective-permute-start(bf16[4,16,1,4,128]{4,3,0,1,2:T(4,128)(2,1)S(1)} %fusion.31), channel_id=1, source_target_pairs={{0,4},{4,0},{8,12},{12,8},{16,20},{20,16},{24,28},{28,24},{32,36},... | collective-permute-start | bytes 196616 | tf_op jit(solution)/shard_map/ppermute | solution.py:41
Sparse Core Ops, SparseCore 0:
  9.4 59.2 all-gather.2
  71.9 132.4 all-gather.4
where the time goes:
time: 257 us; the launch traced here: 256 us
  waiting for transfers between devices  189 us (74%)
  local copies, waits for them, and re-layouts  20.3 us (8%)
  starting transfers between devices  15.2 us (6%)
  between operations  13.7 us (5%)
  blocking collectives  7.99 us (3%)
  matrix products  5.84 us (2%)
  other arithmetic  4.02 us (2%)
    all_gather x1, waiting for transfers between devices, in_one_piece(): whole, at, done = (lax.all_gather(both, axis, axis=dim, tiled=True), 0, [])  119 us
    all_gather x1, waiting for transfers between devices, body(): sec_group = lax.all_gather(hidden_states, 'sec', axis=1, tiled=True)  59 us
    ppermute x5, starting transfers between devices, swapped(): return lax.ppermute(value, axis, pairs)  10.8 us
    all_to_all x1, waiting for transfers between devices, sum_at_owner(): parts = lax.all_to_all(in_blocks(x, dim, length), axis, 0, 0, tiled=True)  9.9 us
    dynamic_slice x1, local copies, waits for them, and re-layouts, body(): lax.dynamic_slice_in_dim(grouped, sec_index, 1, 2)  8.36 us
    all_to_all x1, blocking collectives, body(): lax.all_to_all(attended, 'sec', split_axis=2, concat_axis=1, tiled=True)  7.99 us
    reshape x1, local copies, waits for them, and re-layouts, body(): grouped = sec_group.reshape(group_rows, dp_count, sec_count, shard_rows)  7.89 us
  transfers between devices with their start and end apart: 8, of which 4 were waited for; matrix products, arithmetic and copies ran while one was open for 8% of the time, Pallas kernels for 0%

commit v1 on v0

v1 whole, which is shorter than its diff:
```python
import jax
import jax.numpy as jnp
from jax import lax
from jax.experimental import pallas as pl
from jax.experimental.pallas import tpu as pltpu
from jax.sharding import Mesh, PartitionSpec as P

THETA = 500000.0
NEG = -1e30


def regroup(hidden, groups, pair, width):
    rows = hidden.shape[0]
    xs, secs = groups

    def kernel(h_ref, o_ref, sems):
        copies = []
        for x in range(xs):
            for s in range(secs):
                for h in range(pair):
                    src = ((x * pair + h) * secs + s) * width
                    copies.append(
                        pltpu.make_async_copy(
                            h_ref.at[:, pl.ds(src, width)],
                            o_ref.at[x * secs + s, :, pl.ds(h * width, width)],
                            sems.at[len(copies)],
                        )
                    )
        for c in copies:
            c.start()
        for c in copies:
            c.wait()

    return pl.pallas_call(
        kernel,
        out_shape=jax.ShapeDtypeStruct((xs * secs, rows, pair * width), hidden.dtype),
        in_specs=[pl.BlockSpec(memory_space=pl.ANY)],
        out_specs=pl.BlockSpec(memory_space=pltpu.VMEM),
        scratch_shapes=[pltpu.SemaphoreType.DMA((xs * secs * pair,))],
        cost_estimate=pl.CostEstimate(flops=0, bytes_accessed=2 * hidden.size * 2, transcendentals=0),
        name="regroup",
    )(hidden)


def project(tokens, w_own, k_own, w_other, k_other, half):
    groups, rows, feats = tokens.shape
    width = feats // 2
    q_cols = w_own.shape[1]
    kv_cols = k_own.shape[1]
    step = 4

    def kernel(half_ref, t_ref, wo_ref, ko_ref, wp_ref, kp_ref, o_ref):
        mine = pl.multiple_of(half_ref[0] * width, width)
        theirs = pl.multiple_of((1 - half_ref[0]) * width, width)
        a = t_ref[:, :, pl.ds(mine, width)].reshape(step * rows, width)
        b = t_ref[:, :, pl.ds(theirs, width)].reshape(step * rows, width)
        q = jnp.dot(a, wo_ref[...], preferred_element_type=jnp.float32)
        q = q + jnp.dot(b, wp_ref[...], preferred_element_type=jnp.float32)
        o_ref[:, :, pl.ds(0, q_cols)] = q.astype(jnp.bfloat16).reshape(step, rows, q_cols)
        k = jnp.dot(a, ko_ref[...], preferred_element_type=jnp.float32)
        k = k + jnp.dot(b, kp_ref[...], preferred_element_type=jnp.float32)
        o_ref[:, :, pl.ds(q_cols, kv_cols)] = k.astype(jnp.bfloat16).reshape(step, rows, kv_cols)

    def whole(a):
        return pl.BlockSpec(a.shape, lambda i, h: (0, 0))

    return pl.pallas_call(
        kernel,
        out_shape=jax.ShapeDtypeStruct((groups, rows, q_cols + kv_cols), jnp.bfloat16),
        grid_spec=pltpu.PrefetchScalarGridSpec(
            num_scalar_prefetch=1,
            grid=(groups // step,),
            in_specs=[
                pl.BlockSpec((step, rows, feats), lambda i, h: (i, 0, 0)),
                whole(w_own),
                whole(k_own),
                whole(w_other),
                whole(k_other),
            ],
            out_specs=pl.BlockSpec((step, rows, q_cols + kv_cols), lambda i, h: (i, 0, 0)),
        ),
        name="project",
    )(half, tokens, w_own, k_own, w_other, k_other)


def finish_projection(parts, cosine, sine, parity, heads, steps):
    groups, rows, cols = parts.shape
    size = cosine.shape[1]
    batch = rows // steps

    def kernel(par_ref, p_ref, c_ref, s_ref, q_ref, kv_ref, qf, kvf):
        total = p_ref[0].astype(jnp.float32)
        for g in range(1, groups):
            total = total + p_ref[g].astype(jnp.float32)
        cos = c_ref[...]
        sin = s_ref[...]

        def rope(v):
            return v * cos + pltpu.roll(v, size // 2, 1) * sin

        own = total[:, heads * size :]
        own = jnp.where(par_ref[0] == 0, rope(own), own)
        kvf[...] = own.astype(jnp.bfloat16).astype(jnp.float32)
        for h in range(heads):
            qf[h] = rope(total[:, h * size : (h + 1) * size])
        for b in range(batch):
            kv_ref[b] = kvf[pl.ds(b, steps, stride=batch), :]
            per_head = [qf[h, pl.ds(b, steps, stride=batch), :] for h in range(heads)]
            q_ref[b] = jnp.concatenate(per_head, axis=0).astype(jnp.bfloat16)

    vm = pl.BlockSpec(memory_space=pltpu.VMEM)
    return pl.pallas_call(
        kernel,
        out_shape=(
            jax.ShapeDtypeStruct((batch, heads * steps, size), jnp.bfloat16),
            jax.ShapeDtypeStruct((batch, steps, size), jnp.float32),
        ),
        in_specs=[pl.BlockSpec(memory_space=pltpu.SMEM), vm, vm, vm],
        out_specs=(vm, vm),
        scratch_shapes=[
            pltpu.VMEM((heads, rows, size), jnp.float32),
            pltpu.VMEM((rows, size), jnp.float32),
        ],
        name="finish_projection",
    )(parity, parts, cosine, sine)


def attend(scalars, query, own_kv, other_kv, k_own, k_other, v_own, v_other, steps):
    batch, q_rows, size = query.shape
    heads = q_rows // steps
    half_len = k_own.shape[2]
    scale = size ** (-0.5)
    block = 4
    rows = steps * batch
    nt = (((1,), (1,)), ((), ()))

    def kernel(s_ref, q_ref, mine_ref, theirs_ref, ka_ref, kb_ref, va_ref, vb_ref, o_ref, acc):
        i = pl.program_id(0)
        parity = s_ref[0]
        key_first = parity == 0
        pos = lax.broadcasted_iota(jnp.int32, (q_rows, half_len), 1)
        pos_a = pos + parity * half_len
        pos_b = pos + (1 - parity) * half_len
        step_row = lax.broadcasted_iota(jnp.int32, (q_rows, steps), 0) % steps
        causal = lax.broadcasted_iota(jnp.int32, (q_rows, steps), 1) <= step_row
        for j in range(block):
            b = i * block + j
            begin = s_ref[1 + b]
            end = s_ref[1 + batch + b]
            q = q_ref[j]
            mine = mine_ref[j]
            theirs = theirs_ref[j]
            new_k = jnp.where(key_first, mine, theirs).astype(jnp.bfloat16)
            new_v = jnp.where(key_first, theirs, mine).astype(jnp.bfloat16)
            live_a = (pos_a >= begin) & (pos_a < end)
            live_b = (pos_b >= begin) & (pos_b < end)
            sa = lax.dot_general(q, ka_ref[j, 0], nt, preferred_element_type=jnp.float32) * scale
            sb = lax.dot_general(q, kb_ref[j, 0], nt, preferred_element_type=jnp.float32) * scale
            sn = lax.dot_general(q, new_k, nt, preferred_element_type=jnp.float32) * scale
            sa = jnp.where(live_a, sa, NEG)
            sb = jnp.where(live_b, sb, NEG)
            sn = jnp.where(causal, sn, NEG)
            peak = jnp.maximum(
                jnp.max(jnp.maximum(sa, sb), axis=-1, keepdims=True),
                jnp.max(sn, axis=-1, keepdims=True),
            )
            ea = jnp.where(live_a, jnp.exp(sa - peak), 0.0)
            eb = jnp.where(live_b, jnp.exp(sb - peak), 0.0)
            en = jnp.where(causal, jnp.exp(sn - peak), 0.0)
            total = jnp.sum(ea + eb, axis=-1, keepdims=True) + jnp.sum(en, axis=-1, keepdims=True)
            w = jnp.dot(ea.astype(jnp.bfloat16), va_ref[j, 0], preferred_element_type=jnp.float32)
            w = w + jnp.dot(eb.astype(jnp.bfloat16), vb_ref[j, 0], preferred_element_type=jnp.float32)
            w = w + jnp.dot(en.astype(jnp.bfloat16), new_v, preferred_element_type=jnp.float32)
            w = w / total
            for h in range(heads):
                acc[pl.ds(h * rows + b, steps, stride=batch), :] = w[h * steps : (h + 1) * steps]

        @pl.when(i == pl.num_programs(0) - 1)
        def _():
            o_ref[...] = acc[...].astype(jnp.bfloat16).reshape(heads, rows, size)

    def per(a):
        return pl.BlockSpec((block,) + a.shape[1:], lambda i, s: (i,) + (0,) * (a.ndim - 1))

    return pl.pallas_call(
        kernel,
        out_shape=jax.ShapeDtypeStruct((heads, rows, size), jnp.bfloat16),
        grid_spec=pltpu.PrefetchScalarGridSpec(
            num_scalar_prefetch=1,
            grid=(batch // block,),
            in_specs=[per(a) for a in (query, own_kv, other_kv, k_own, k_other, v_own, v_other)],
            out_specs=pl.BlockSpec((heads, rows, size), lambda i, s: (0, 0, 0)),
            scratch_shapes=[pltpu.VMEM((heads * rows, size), jnp.float32)],
        ),
        name="attend",
    )(scalars, query, own_kv, other_kv, k_own, k_other, v_own, v_other)


def body(hidden_states, w_query, w_keyval, key_cache, value_cache, cache_begin, cache_end):
    steps, batch, width = hidden_states.shape
    size = key_cache.shape[-1]
    heads = w_query.shape[1] // size
    xs, zs, secs = lax.axis_size("x"), lax.axis_size("zh"), lax.axis_size("sec")
    half = lax.axis_index("zh").astype(jnp.int32)
    parity = lax.axis_index("core").astype(jnp.int32)
    swap = [(0, 1), (1, 0)]

    w_other = lax.ppermute(w_query, "zh", swap)
    k_other = lax.ppermute(w_keyval, "zh", swap)
    keys_other = lax.ppermute(key_cache, "core", swap)
    values_other = lax.ppermute(value_cache, "core", swap)

    grouped = regroup(
        hidden_states.reshape(steps * batch, width), (xs, secs), zs, w_query.shape[0]
    )
    tokens = lax.all_to_all(grouped, ("x", "sec"), 0, 0, tiled=True)
    partial = project(tokens, w_query, w_keyval, w_other, k_other, half.reshape(1))
    parts = lax.all_to_all(partial, ("x", "sec"), 0, 0, tiled=True)

    position = (
        cache_end.astype(jnp.float32)[None, :] + jnp.arange(steps, dtype=jnp.float32)[:, None]
    ).reshape(steps * batch, 1)
    freq = THETA ** (-(jnp.arange(size // 2, dtype=jnp.float32) * 2.0 / size))
    angle = position * freq
    cosine = jnp.cos(angle)
    sine = jnp.sin(angle)
    cosine = jnp.concatenate([cosine, cosine], axis=1)
    sine = jnp.concatenate([-sine, sine], axis=1)

    query, own_kv = finish_projection(parts, cosine, sine, parity.reshape(1), heads, steps)
    other_kv = lax.ppermute(own_kv, "core", swap)
    scalars = jnp.concatenate([parity.reshape(1), cache_begin, cache_end])
    attended = attend(
        scalars, query, own_kv, other_kv, key_cache, keys_other, value_cache, values_other, steps
    )
    handed = lax.all_to_all(attended, "sec", 0, 0, tiled=True)
    handed = handed.reshape(secs, steps, batch, size)
    return jnp.transpose(handed, (1, 0, 2, 3)).reshape(steps, secs * batch, size)


def solution(mesh):
    dp, tp, sec = (mesh.shape[a] for a in ("dp", "tp", "sec"))
    fine = Mesh(mesh.devices.reshape(dp // 2, 2, tp // 2, 2, sec), ("x", "zh", "zl", "core", "sec"))
    rows, cols = ("x", "zh", "sec"), ("zl", "core")
    return jax.shard_map(
        body,
        mesh=fine,
        in_specs=(
            P(None, rows, None),
            P(rows, cols),
            P(rows, cols),
            P(rows, cols, None, None),
            P(rows, cols, None, None),
            P(rows),
            P(rows),
        ),
        out_specs=P(None, ("x", "zh"), ("zl", "core", "sec")),
        check_vma=False,
    )
```

time: 257 us -> 109 us (0.42)
  the two profiles are of different devices: /device:TPU:96 before, /device:TPU:32 now
where the time goes in v1:
time: 109 us
  waiting for transfers between devices  41.2 us (38%)
  starting transfers between devices  37.2 us (34%)
  Pallas kernels  16.2 us (15%)
  blocking collectives  8.87 us (8%)
  local copies, waits for them, and re-layouts  3.5 us (3%)
  other arithmetic  1.53 us (1%)
    ppermute x1, waiting for transfers between devices, body(): k_other = lax.ppermute(w_keyval, 'zh', swap)  26.4 us
    ppermute x1, starting transfers between devices, body(): w_other = lax.ppermute(w_query, 'zh', swap)  14.8 us
    all_to_all x1, waiting for transfers between devices, body(): parts = lax.all_to_all(partial, ('x', 'sec'), 0, 0, tiled=True)  14 us
    all_to_all x1, blocking collectives, body(): handed = lax.all_to_all(attended, 'sec', 0, 0, tiled=True)  8.87 us
    all_to_all x1, starting transfers between devices, body(): tokens = lax.all_to_all(grouped, ('x', 'sec'), 0, 0, tiled=True)  7.18 us
    pallas_call x1, Pallas kernels, attend(): pl.pallas_call(kernel, out_shape=jax.ShapeDtypeStruct((heads, rows, size)...  7.14 us
    all_to_all x1, starting transfers between devices, body(): parts = lax.all_to_all(partial, ('x', 'sec'), 0, 0, tiled=True)  7.08 us
    pallas_call x1, Pallas kernels, project(): pl.pallas_call(kernel, out_shape=jax.ShapeDtypeStruct((groups, rows, q_co...  4.31 us
  transfers between devices with their start and end apart: 7, of which 3 were waited for; matrix products, arithmetic and copies ran while one was open for 1% of the time, Pallas kernels for 2%

profile of v1, /device:TPU:32, one launch (start us, length us, event | category | flops | bytes accessed | tf_op | source)
XLA Modules:
  0.0 108.6 jit_solution(16376081456925863637)
XLA Ops:
  0.0 2.5 %regroup.1 = bf16[16,64,512]{2,1,0:T(8,128)(2,1)} custom-call(bf16[64,8192]{1,0:T(8,128)(2,1)} %bitcast.7), custom_call_target="tpu_custom_call" | custom-call | bytes 2097152 | tf_op jit(solution)/shard_map/regroup/pallas_call | solution.py:34
  2.5 7.2 %all-to-all-start = ((bf16[16,64,512]{2,1,0:T(8,128)(2,1)}), bf16[16,64,512]{2,1,0:T(8,128)(2,1)S(1)}, u32[]{:S(2)}, u32[]{:S(2)}) async-start(bf16[16,64,512]{2,1,0:T(8,128)(2,1)} %regroup.1), calls=%async_computation | async-start | bytes 2097152 | tf_op jit(solution)/shard_map/all_to_all | solution.py:216
  9.7 14.8 %collective-permute-start = (bf16[256,512]{1,0:T(8,128)(2,1)S(1)}, bf16[256,512]{1,0:T(8,128)(2,1)S(1)}, u32[]{:S(2)}, u32[]{:S(2)}) collective-permute-start(bf16[256,512]{1,0:T(8,128)(2,1)S(1)} %copy-done.4), channel_id=1, source_target_pairs={{0,64},{64,0},{1,65},{65,1},{2,66},{66,2},{3,67},{67,3},{4,68},{68... | collective-permute-start | bytes 786440 | tf_op jit(solution)/shard_map/ppermute | solution.py:208
  24.5 1.9 %collective-permute-start.1 = (bf16[256,128]{1,0:T(8,128)(2,1)S(1)}, bf16[256,128]{1,0:T(8,128)(2,1)S(1)}, u32[]{:S(2)}, u32[]{:S(2)}) collective-permute-start(bf16[256,128]{1,0:T(8,128)(2,1)S(1)} %copy-done.6), channel_id=1, source_target_pairs={{0,64},{64,0},{1,65},{65,1},{2,66},{66,2},{3,67},{67,3},{4,68},{68... | collective-permute-start | bytes 196616 | tf_op jit(solution)/shard_map/ppermute | solution.py:209
  26.5 26.4 %collective-permute-done.1.kp_ref = bf16[256,128]{1,0:T(8,128)(2,1)S(1)} collective-permute-done((bf16[256,128]{1,0:T(8,128)(2,1)S(1)}, bf16[256,128]{1,0:T(8,128)(2,1)S(1)}, u32[]{:S(2)}, u32[]{:S(2)}) %collective-permute-start.1) | collective-permute-done | bytes 65568 | tf_op jit(solution)/shard_map/ppermute | solution.py:209
  52.9 0.6 copy-done.7
  53.5 0.1 copy-done.5
  53.5 0.4 copy-done.1
  53.9 4.3 %project.1 = bf16[16,64,640]{2,1,0:T(8,128)(2,1)} custom-call(s32[1]{0:T(128)} %bitcast.1.half_ref, bf16[16,64,512]{2,1,0:T(8,128)(2,1)} %copy-done.1, bf16[256,512]{1,0:T(8,128)(2,1)} %wo_ref.1, bf16[256,128]{1,0:T(8,128)(2,1)} %ko_ref.1, bf16[256,512]{1,0:T(8,128)(2,1)} %copy-done.5, bf16[256,128]{1,0:T(8,128)(2,1)} %copy-done.7), custom_call_target="tpu_custom_call" | custom-call | tf_op jit(solution)/shard_map/project/pallas_call | solution.py:67
  58.2 7.1 %all-to-all-start.1 = ((bf16[16,64,640]{2,1,0:T(8,128)(2,1)}), bf16[16,64,640]{2,1,0:T(8,128)(2,1)S(1)}, u32[]{:S(2)}, u32[]{:S(2)}) async-start(bf16[16,64,640]{2,1,0:T(8,128)(2,1)} %project.1), calls=%async_computation.1 | async-start | bytes 2621440 | tf_op jit(solution)/shard_map/all_to_all | solution.py:218
  65.3 1.9 %collective-permute-start.3 = (bf16[16,1,256,128]{3,2,1,0:T(8,128)(2,1)S(1)}, bf16[16,1,256,128]{3,2,1,0:T(8,128)(2,1)}, u32[]{:S(2)}, u32[]{:S(2)}) collective-permute-start(bf16[16,1,256,128]{3,2,1,0:T(8,128)(2,1)S(1)} %copy-done.2), channel_id=1, source_target_pairs={{0,4},{4,0},{1,5},{5,1},{2,6},{6,2},{3,7},{7,3},{8,12},{12,8},{9,1... | collective-permute-start | bytes 3145736 | tf_op jit(solution)/shard_map/ppermute | solution.py:210
  67.3 2.4 %collective-permute-start.4 = (bf16[16,1,256,128]{3,2,1,0:T(8,128)(2,1)S(1)}, bf16[16,1,256,128]{3,2,1,0:T(8,128)(2,1)}, u32[]{:S(2)}, u32[]{:S(2)}) collective-permute-start(bf16[16,1,256,128]{3,2,1,0:T(8,128)(2,1)S(1)} %copy-done.3), channel_id=1, source_target_pairs={{0,4},{4,0},{1,5},{5,1},{2,6},{6,2},{3,7},{7,3},{8,12},{12,8},{9,1... | collective-permute-start | bytes 3145736 | tf_op jit(solution)/shard_map/ppermute | solution.py:211
  69.8 0.2 fusion
  70.0 0.7 pad_maximum_fusion
  70.8 14.0 %all-to-all-done.1.p_ref = bf16[16,64,640]{2,1,0:T(8,128)(2,1)S(1)} async-done(((bf16[16,64,640]{2,1,0:T(8,128)(2,1)}), bf16[16,64,640]{2,1,0:T(8,128)(2,1)S(1)}, u32[]{:S(2)}, u32[]{:S(2)}) %all-to-all-start.1) | async-done | bytes 1310752 | tf_op jit(solution)/shard_map/all_to_all | solution.py:218
  84.8 1.1 copy-done
  85.8 2.2 %finish_projection.1 = (bf16[16,16,128]{2,1,0:T(8,128)(2,1)}, f32[16,4,128]{2,1,0:T(4,128)}) custom-call(s32[1]{0:T(128)} %bitcast.par_ref, bf16[16,64,640]{2,1,0:T(8,128)(2,1)} %copy-done, f32[64,128]{1,0:T(8,128)} %get-tuple-element.12.c_ref, f32[64,128]{1,0:T(8,128)} %get-tuple-element.13.s_ref), custom_call_target="tpu_custom_call" | custom-call | tf_op jit(solution)/shard_map/finish_projection/pallas_call | solution.py:112
  88.1 1.9 %collective-permute-start.2 = (f32[16,4,128]{2,1,0:T(4,128)}, f32[16,4,128]{2,1,0:T(4,128)S(1)}, u32[]{:S(2)}, u32[]{:S(2)}) collective-permute-start(f32[16,4,128]{2,1,0:T(4,128)} %get-tuple-element.8.mine_ref), channel_id=1, source_target_pairs={{0,4},{4,0},{1,5},{5,1},{2,6},{6,2},{3,7},{7,3},{8,12},{12,8},{9,1... | collective-permute-start | bytes 98312 | tf_op jit(solution)/shard_map/ppermute | solution.py:231
  90.0 0.6 pad_add_fusion.s_ref
  90.6 0.8 collective-permute-done.2.theirs_ref
  91.4 0.6 copy-done.8
  92.0 7.1 %attend.1 = bf16[4,64,128]{2,1,0:T(8,128)(2,1)} custom-call(s32[33]{0:T(128)} %pad_add_fusion.s_ref, bf16[16,16,128]{2,1,0:T(8,128)(2,1)} %get-tuple-element.7.q_ref, f32[16,4,128]{2,1,0:T(4,128)} %get-tuple-element.8.mine_ref, f32[16,4,128]{2,1,0:T(4,128)} %copy-done.8, bf16[16,1,256,128]{3,2,1,0:T(8,128)(2,1)} %ka_ref.1, ...), custom_call_target="tpu_custom_call" | custom-call | tf_op jit(solution)/shard_map/attend/pallas_call | solution.py:185
  99.1 8.9 %all_to_all.15 = bf16[4,64,128]{2,1,0:T(8,128)(2,1)S(1)} all-to-all(bf16[4,64,128]{2,1,0:T(8,128)(2,1)} %attend.1), channel_id=1, replica_groups=mesh['x'=4,'zh'=2,'zl'=8,'core'=2,'sec'=4] {'sec'}, dimensions={0} | all-to-all | bytes 131072 | tf_op jit(solution)/shard_map/all_to_all | solution.py:236
  108.0 0.6 copy.8
  (25 shorter events, 0.2 us)
Async XLA Ops:
  2.5 7.2 %copy-start.4 = (bf16[256,512]{1,0:T(8,128)(2,1)S(1)}, bf16[256,512]{1,0:T(8,128)(2,1)}, u32[]{:S(2)}) copy-start(bf16[256,512]{1,0:T(8,128)(2,1)} %wo_ref.1) | copy-start | bytes 786436
  2.5 22.0 %copy-start.6 = (bf16[256,128]{1,0:T(8,128)(2,1)S(1)}, bf16[256,128]{1,0:T(8,128)(2,1)}, u32[]{:S(2)}) copy-start(bf16[256,128]{1,0:T(8,128)(2,1)} %ko_ref.1) | copy-start | bytes 196612
  2.5 50.4 %all-to-all-start = ((bf16[16,64,512]{2,1,0:T(8,128)(2,1)}), bf16[16,64,512]{2,1,0:T(8,128)(2,1)S(1)}, u32[]{:S(2)}, u32[]{:S(2)}) async-start(bf16[16,64,512]{2,1,0:T(8,128)(2,1)} %regroup.1), calls=%async_computation | async-start | bytes 2097152 | tf_op jit(solution)/shard_map/all_to_all | solution.py:216
  9.7 43.1 %collective-permute-start = (bf16[256,512]{1,0:T(8,128)(2,1)S(1)}, bf16[256,512]{1,0:T(8,128)(2,1)S(1)}, u32[]{:S(2)}, u32[]{:S(2)}) collective-permute-start(bf16[256,512]{1,0:T(8,128)(2,1)S(1)} %copy-done.4), channel_id=1, source_target_pairs={{0,64},{64,0},{1,65},{65,1},{2,66},{66,2},{3,67},{67,3},{4,68},{68... | collective-permute-start | bytes 786440 | tf_op jit(solution)/shard_map/ppermute | solution.py:208
  24.5 28.3 %collective-permute-start.1 = (bf16[256,128]{1,0:T(8,128)(2,1)S(1)}, bf16[256,128]{1,0:T(8,128)(2,1)S(1)}, u32[]{:S(2)}, u32[]{:S(2)}) collective-permute-start(bf16[256,128]{1,0:T(8,128)(2,1)S(1)} %copy-done.6), channel_id=1, source_target_pairs={{0,64},{64,0},{1,65},{65,1},{2,66},{66,2},{3,67},{67,3},{4,68},{68... | collective-permute-start | bytes 196616 | tf_op jit(solution)/shard_map/ppermute | solution.py:209
  52.8 0.6 copy-start.7
  52.8 0.7 copy-start.5
  52.8 1.1 copy-start.1
  58.2 7.1 %copy-start.2 = (bf16[16,1,256,128]{3,2,1,0:T(8,128)(2,1)S(1)}, bf16[16,1,256,128]{3,2,1,0:T(8,128)(2,1)}, u32[]{:S(2)}) copy-start(bf16[16,1,256,128]{3,2,1,0:T(8,128)(2,1)} %ka_ref.1) | copy-start | bytes 3145732
  58.2 9.1 %copy-start.3 = (bf16[16,1,256,128]{3,2,1,0:T(8,128)(2,1)S(1)}, bf16[16,1,256,128]{3,2,1,0:T(8,128)(2,1)}, u32[]{:S(2)}) copy-start(bf16[16,1,256,128]{3,2,1,0:T(8,128)(2,1)} %va_ref.1) | copy-start | bytes 3145732
  58.2 11.5 %copy-start.9 = (s32[16]{0:T(128)S(1)}, s32[16]{0:T(128)}, u32[]{:S(2)}) copy-start(s32[16]{0:T(128)} %param.13) | copy-start | bytes 196
  58.2 26.5 %all-to-all-start.1 = ((bf16[16,64,640]{2,1,0:T(8,128)(2,1)}), bf16[16,64,640]{2,1,0:T(8,128)(2,1)S(1)}, u32[]{:S(2)}, u32[]{:S(2)}) async-start(bf16[16,64,640]{2,1,0:T(8,128)(2,1)} %project.1), calls=%async_computation.1 | async-start | bytes 2621440 | tf_op jit(solution)/shard_map/all_to_all | solution.py:218
  65.3 24.7 %copy-start.10 = (s32[16]{0:T(128)S(1)}, s32[16]{0:T(128)}, u32[]{:S(2)}) copy-start(s32[16]{0:T(128)} %param.12) | copy-start | bytes 196
  65.3 25.3 %collective-permute-start.3 = (bf16[16,1,256,128]{3,2,1,0:T(8,128)(2,1)S(1)}, bf16[16,1,256,128]{3,2,1,0:T(8,128)(2,1)}, u32[]{:S(2)}, u32[]{:S(2)}) collective-permute-start(bf16[16,1,256,128]{3,2,1,0:T(8,128)(2,1)S(1)} %copy-done.2), channel_id=1, source_target_pairs={{0,4},{4,0},{1,5},{5,1},{2,6},{6,2},{3,7},{7,3},{8,12},{12,8},{9,1... | collective-permute-start | bytes 3145736 | tf_op jit(solution)/shard_map/ppermute | solution.py:210
  67.3 23.3 %collective-permute-start.4 = (bf16[16,1,256,128]{3,2,1,0:T(8,128)(2,1)S(1)}, bf16[16,1,256,128]{3,2,1,0:T(8,128)(2,1)}, u32[]{:S(2)}, u32[]{:S(2)}) collective-permute-start(bf16[16,1,256,128]{3,2,1,0:T(8,128)(2,1)S(1)} %copy-done.3), channel_id=1, source_target_pairs={{0,4},{4,0},{1,5},{5,1},{2,6},{6,2},{3,7},{7,3},{8,12},{12,8},{9,1... | collective-permute-start | bytes 3145736 | tf_op jit(solution)/shard_map/ppermute | solution.py:211
  84.8 1.1 copy-start
  88.1 3.3 %collective-permute-start.2 = (f32[16,4,128]{2,1,0:T(4,128)}, f32[16,4,128]{2,1,0:T(4,128)S(1)}, u32[]{:S(2)}, u32[]{:S(2)}) collective-permute-start(f32[16,4,128]{2,1,0:T(4,128)} %get-tuple-element.8.mine_ref), channel_id=1, source_target_pairs={{0,4},{4,0},{1,5},{5,1},{2,6},{6,2},{3,7},{7,3},{8,12},{12,8},{9,1... | collective-permute-start | bytes 98312 | tf_op jit(solution)/shard_map/ppermute | solution.py:231
  91.4 0.6 copy-start.8

commit v2 on v1

v2 whole, which is shorter than its diff:
```python
import jax
import jax.numpy as jnp
from jax import lax
from jax.experimental import pallas as pl
from jax.experimental.pallas import tpu as pltpu
from jax.sharding import Mesh, PartitionSpec as P

THETA = 500000.0
NEG = -1e30


def limits(mib):
    return pltpu.CompilerParams(vmem_limit_bytes=mib << 20)


def regroup(hidden, w_query, w_keyval, groups, pair):
    rows = hidden.shape[0]
    xs, secs = groups
    width, q_cols = w_query.shape
    kv_cols = w_keyval.shape[1]

    def kernel(h_ref, q_ref, k_ref, o_ref, w_ref, sems):
        copies = []

        def add(src, dst):
            copies.append(pltpu.make_async_copy(src, dst, sems.at[len(copies)]))

        for x in range(xs):
            for s in range(secs):
                for h in range(pair):
                    at = ((x * pair + h) * secs + s) * width
                    add(
                        h_ref.at[:, pl.ds(at, width)],
                        o_ref.at[x * secs + s, :, pl.ds(h * width, width)],
                    )
        add(q_ref, w_ref.at[:, pl.ds(0, q_cols)])
        add(k_ref, w_ref.at[:, pl.ds(q_cols, kv_cols)])
        for c in copies:
            c.start()
        for c in copies:
            c.wait()

    hbm = pl.BlockSpec(memory_space=pl.ANY)
    vm = pl.BlockSpec(memory_space=pltpu.VMEM)
    return pl.pallas_call(
        kernel,
        out_shape=(
            jax.ShapeDtypeStruct((xs * secs, rows, pair * width), hidden.dtype),
            jax.ShapeDtypeStruct((width, q_cols + kv_cols), w_query.dtype),
        ),
        in_specs=[hbm, hbm, hbm],
        out_specs=(vm, vm),
        scratch_shapes=[pltpu.SemaphoreType.DMA((xs * secs * pair + 2,))],
        name="regroup",
    )(hidden, w_query, w_keyval)


def project(half, tokens, w_own, w_other):
    groups, rows, feats = tokens.shape
    width, cols = w_own.shape
    step = 4

    def kernel(half_ref, t_ref, wo_ref, wp_ref, o_ref):
        mine = pl.multiple_of(half_ref[0] * width, width)
        theirs = pl.multiple_of((1 - half_ref[0]) * width, width)
        for g in range(0, groups, step):
            a = t_ref[g : g + step, :, pl.ds(mine, width)].reshape(step * rows, width)
            b = t_ref[g : g + step, :, pl.ds(theirs, width)].reshape(step * rows, width)
            y = jnp.dot(a, wo_ref[...], preferred_element_type=jnp.float32)
            y = y + jnp.dot(b, wp_ref[...], preferred_element_type=jnp.float32)
            o_ref[g : g + step] = y.astype(jnp.bfloat16).reshape(step, rows, cols)

    vm = pl.BlockSpec(memory_space=pltpu.VMEM)
    return pl.pallas_call(
        kernel,
        out_shape=jax.ShapeDtypeStruct((groups, rows, cols), jnp.bfloat16),
        in_specs=[pl.BlockSpec(memory_space=pltpu.SMEM), vm, vm, vm],
        out_specs=vm,
        compiler_params=limits(16),
        name="project",
    )(half, tokens, w_own, w_other)


def reorder(n, batch, heads, steps, to_batch):
    a = lax.broadcasted_iota(jnp.int32, (n, n), 0 if to_batch else 1)
    c = lax.broadcasted_iota(jnp.int32, (n, n), 1 if to_batch else 0)
    from_a = (a % (heads * steps)) * batch + a // (heads * steps)
    return (from_a == c).astype(jnp.float32).astype(jnp.bfloat16)


def finish_projection(parity, parts, cosine, sine, heads, steps):
    groups, rows, _ = parts.shape
    size = cosine.shape[1]
    batch = rows // steps

    def kernel(par_ref, p_ref, c_ref, s_ref, q_ref, kv_ref):
        cos = c_ref[...]
        sin = s_ref[...]

        def rope(v):
            return v * cos + pltpu.roll(v, size // 2, 1) * sin

        def summed(h):
            total = p_ref[0, :, h * size : (h + 1) * size].astype(jnp.float32)
            for g in range(1, groups):
                total = total + p_ref[g, :, h * size : (h + 1) * size].astype(jnp.float32)
            return total

        own = summed(heads)
        kv_ref[...] = jnp.where(par_ref[0] == 0, rope(own), own).astype(jnp.bfloat16)
        q = jnp.concatenate([rope(summed(h)).astype(jnp.bfloat16) for h in range(heads)], axis=0)
        order = reorder(heads * rows, batch, heads, steps, True)
        q_ref[...] = jnp.dot(order, q, preferred_element_type=jnp.float32).astype(jnp.bfloat16)

    vm = pl.BlockSpec(memory_space=pltpu.VMEM)
    return pl.pallas_call(
        kernel,
        out_shape=(
            jax.ShapeDtypeStruct((heads * rows, size), jnp.bfloat16),
            jax.ShapeDtypeStruct((rows, size), jnp.bfloat16),
        ),
        in_specs=[pl.BlockSpec(memory_space=pltpu.SMEM), vm, vm, vm],
        out_specs=(vm, vm),
        compiler_params=limits(16),
        name="finish_projection",
    )(parity, parts, cosine, sine)


def attend(parity, begin, end, query, own_kv, other_kv, k_own, k_other, v_own, v_other, steps):
    n, size = query.shape
    rows = own_kv.shape[0]
    batch = rows // steps
    per = n // batch
    heads = per // steps
    half_len = k_own.shape[2]
    scale = size ** (-0.5)
    block = 4
    nt = (((1,), (1,)), ((), ()))

    def kernel(
        par_ref, begin_ref, end_ref, q_ref, mine_ref, theirs_ref, ka, kb, va, vb, o_ref
    ):
        key_first = par_ref[0] == 0
        offset_a = par_ref[0] * half_len
        offset_b = half_len - offset_a
        new_k = jnp.where(key_first, mine_ref[...], theirs_ref[...])
        new_v = jnp.where(key_first, theirs_ref[...], mine_ref[...])
        pos = lax.broadcasted_iota(jnp.int32, (per, half_len), 1)
        done = []
        for i in range(0, batch, block):
            lo, m = i * per, block * per
            q = q_ref[lo : lo + m]
            sa, sb = [], []
            for b in range(i, i + block):
                qb = q_ref[b * per : (b + 1) * per]
                for keys, offset, out in ((ka, offset_a, sa), (kb, offset_b, sb)):
                    s = lax.dot_general(qb, keys[b, 0], nt, preferred_element_type=jnp.float32)
                    live = (pos >= begin_ref[b] - offset) & (pos < end_ref[b] - offset)
                    out.append(jnp.where(live, s * scale, NEG))
            sa = jnp.concatenate(sa, axis=0)
            sb = jnp.concatenate(sb, axis=0)
            sn = lax.dot_general(q, new_k, nt, preferred_element_type=jnp.float32) * scale
            r = lax.broadcasted_iota(jnp.int32, (m, rows), 0) + lo
            c = lax.broadcasted_iota(jnp.int32, (m, rows), 1)
            seen = (c % batch == r // per) & (c // batch <= r % steps)
            sn = jnp.where(seen, sn, NEG)
            peak = jnp.maximum(
                jnp.max(jnp.maximum(sa, sb), axis=-1, keepdims=True),
                jnp.max(sn, axis=-1, keepdims=True),
            )
            ea = jnp.exp(sa - peak)
            eb = jnp.exp(sb - peak)
            en = jnp.exp(sn - peak)
            total = jnp.sum(ea + eb, axis=-1, keepdims=True) + jnp.sum(en, axis=-1, keepdims=True)
            ea = ea.astype(jnp.bfloat16)
            eb = eb.astype(jnp.bfloat16)
            w = []
            for j in range(block):
                part = slice(j * per, (j + 1) * per)
                wa = jnp.dot(ea[part], va[i + j, 0], preferred_element_type=jnp.float32)
                wb = jnp.dot(eb[part], vb[i + j, 0], preferred_element_type=jnp.float32)
                w.append(wa + wb)
            w = jnp.concatenate(w, axis=0)
            w = w + jnp.dot(en.astype(jnp.bfloat16), new_v, preferred_element_type=jnp.float32)
            done.append((w / total).astype(jnp.bfloat16))
        order = reorder(n, batch, heads, steps, False)
        out = jnp.dot(order, jnp.concatenate(done, axis=0), preferred_element_type=jnp.float32)
        o_ref[...] = out.astype(jnp.bfloat16).reshape(heads, rows, size)

    vm = pl.BlockSpec(memory_space=pltpu.VMEM)
    sm = pl.BlockSpec(memory_space=pltpu.SMEM)
    return pl.pallas_call(
        kernel,
        out_shape=jax.ShapeDtypeStruct((heads, rows, size), jnp.bfloat16),
        in_specs=[sm] * 3 + [vm] * 7,
        out_specs=vm,
        compiler_params=limits(24),
        name="attend",
    )(parity, begin, end, query, own_kv, other_kv, k_own, k_other, v_own, v_other)


def body(hidden_states, w_query, w_keyval, key_cache, value_cache, cache_begin, cache_end):
    steps, batch, width = hidden_states.shape
    size = key_cache.shape[-1]
    heads = w_query.shape[1] // size
    xs, zs, secs = lax.axis_size("x"), lax.axis_size("zh"), lax.axis_size("sec")
    half = lax.axis_index("zh").astype(jnp.int32).reshape(1)
    parity = lax.axis_index("core").astype(jnp.int32).reshape(1)
    swap = [(0, 1), (1, 0)]

    grouped, w_own = regroup(
        hidden_states.reshape(steps * batch, width), w_query, w_keyval, (xs, secs), zs
    )
    keys_other = lax.ppermute(key_cache, "core", swap)
    values_other = lax.ppermute(value_cache, "core", swap)
    tokens = lax.all_to_all(grouped, ("x", "sec"), 0, 0, tiled=True)
    w_other = lax.ppermute(w_own, "zh", swap)
    partial = project(half, tokens, w_own, w_other)
    parts = lax.all_to_all(partial, ("x", "sec"), 0, 0, tiled=True)

    position = (
        cache_end.astype(jnp.float32)[None, :] + jnp.arange(steps, dtype=jnp.float32)[:, None]
    ).reshape(steps * batch, 1)
    freq = THETA ** (-(jnp.arange(size // 2, dtype=jnp.float32) * 2.0 / size))
    angle = position * freq
    cosine = jnp.cos(angle)
    sine = jnp.sin(angle)
    cosine = jnp.concatenate([cosine, cosine], axis=1)
    sine = jnp.concatenate([-sine, sine], axis=1)

    query, own_kv = finish_projection(parity, parts, cosine, sine, heads, steps)
    other_kv = lax.ppermute(own_kv, "core", swap)
    attended = attend(
        parity,
        cache_begin,
        cache_end,
        query,
        own_kv,
        other_kv,
        key_cache,
        keys_other,
        value_cache,
        values_other,
        steps,
    )
    handed = lax.all_to_all(attended, "sec", 0, 0, tiled=True)
    handed = handed.reshape(secs, steps, batch, size)
    return jnp.transpose(handed, (1, 0, 2, 3)).reshape(steps, secs * batch, size)


def solution(mesh):
    dp, tp, sec = (mesh.shape[a] for a in ("dp", "tp", "sec"))
    fine = Mesh(mesh.devices.reshape(dp // 2, 2, tp // 2, 2, sec), ("x", "zh", "zl", "core", "sec"))
    rows, cols = ("x", "zh", "sec"), ("zl", "core")
    return jax.shard_map(
        body,
        mesh=fine,
        in_specs=(
            P(None, rows, None),
            P(rows, cols),
            P(rows, cols),
            P(rows, cols, None, None),
            P(rows, cols, None, None),
            P(rows),
            P(rows),
        ),
        out_specs=P(None, ("x", "zh"), ("zl", "core", "sec")),
        check_vma=False,
    )
```

time: 109 us -> 97.8 us (0.90)
  Pallas kernels: 16.2 us -> 8.74 us
  waiting for transfers between devices: 41.2 us -> 44 us
  local copies, waits for them, and re-layouts: 3.5 us -> 0.74 us
  starting transfers between devices: 37.2 us -> 35.3 us
  other arithmetic: 1.53 us -> 0.31 us
    pallas_call x3, Pallas kernels: 9.01 us -> 5.24 us  [the longest x1 2.81 us: regroup(): pl.pallas_call(kernel, out_shape=(jax.ShapeDtypeStruct((xs * secs, rows,...]
    pallas_call x1, Pallas kernels: 7.14 us -> 3.5 us  [attend(): pl.pallas_call(kernel, out_shape=jax.ShapeDtypeStruct((heads, rows, size)...]
    unnamed x22 -> x10, local copies, waits for them, and re-layouts: 2.78 us -> 0.02 us
    ppermute x2 -> x1, starting transfers between devices: 16.7 us -> 14.8 us  [body(): w_other = lax.ppermute(w_own, 'zh', swap)]
    ppermute x2 -> x1, waiting for transfers between devices: 26.4 us -> 28.3 us  [body(): w_other = lax.ppermute(w_own, 'zh', swap)]
  transfers between devices with their start and end apart: 7 -> 6, of which waited for: 3 -> 3; matrix products, arithmetic and copies ran while one was open for 1% -> 0% of each run, Pallas kernels for 2% -> 0%
where the time goes in v2:
time: 97.8 us; the launch traced here: 97.3 us
  waiting for transfers between devices  44 us (45%)
  starting transfers between devices  35.3 us (36%)
  Pallas kernels  8.74 us (9%)
  blocking collectives  7.99 us (8%)
    ppermute x1, waiting for transfers between devices, body(): w_other = lax.ppermute(w_own, 'zh', swap)  28.3 us
    ppermute x1, starting transfers between devices, body(): w_other = lax.ppermute(w_own, 'zh', swap)  14.8 us
    all_to_all x1, waiting for transfers between devices, body(): parts = lax.all_to_all(partial, ('x', 'sec'), 0, 0, tiled=True)  14.6 us
    all_to_all x1, blocking collectives, body(): handed = lax.all_to_all(attended, 'sec', 0, 0, tiled=True)  7.99 us
    all_to_all x1, starting transfers between devices, body(): tokens = lax.all_to_all(grouped, ('x', 'sec'), 0, 0, tiled=True)  7.18 us
    all_to_all x1, starting transfers between devices, body(): parts = lax.all_to_all(partial, ('x', 'sec'), 0, 0, tiled=True)  7.07 us
    pallas_call x1, Pallas kernels, attend(): pl.pallas_call(kernel, out_shape=jax.ShapeDtypeStruct((heads, rows, size)...  3.5 us
    pallas_call x1, Pallas kernels, regroup(): pl.pallas_call(kernel, out_shape=(jax.ShapeDtypeStruct((xs * secs, rows,...  2.81 us
  transfers between devices with their start and end apart: 6, of which 3 were waited for; matrix products, arithmetic and copies ran while one was open for 0% of the time, Pallas kernels for 0%

profile of v2, /device:TPU:32, one launch (start us, length us, event | category | flops | bytes accessed | tf_op | source)
XLA Modules:
  0.0 97.3 jit_solution(10590658992158428068)
XLA Ops:
  0.0 2.8 %regroup.1 = (bf16[16,64,512]{2,1,0:T(8,128)(2,1)}, bf16[256,640]{1,0:T(8,128)(2,1)}) custom-call(bf16[64,8192]{1,0:T(8,128)(2,1)} %bitcast.7, bf16[256,512]{1,0:T(8,128)(2,1)} %q_ref.1, bf16[256,128]{1,0:T(8,128)(2,1)} %k_ref.1), custom_call_target="tpu_custom_call" | custom-call | tf_op jit(solution)/shard_map/regroup/pallas_call | solution.py:45
  2.8 0.0 copy-start.2
  2.8 7.2 %all-to-all-start = ((bf16[16,64,512]{2,1,0:T(8,128)(2,1)}), bf16[16,64,512]{2,1,0:T(8,128)(2,1)S(1)}, u32[]{:S(2)}, u32[]{:S(2)}) async-start(bf16[16,64,512]{2,1,0:T(8,128)(2,1)} %get-tuple-element.9), calls=%async_computation | async-start | bytes 2097152 | tf_op jit(solution)/shard_map/all_to_all | solution.py:216
  10.0 0.0 copy-done.2
  10.0 14.8 %collective-permute-start = (bf16[256,640]{1,0:T(8,128)(2,1)S(1)}, bf16[256,640]{1,0:T(8,128)(2,1)S(1)}, u32[]{:S(2)}, u32[]{:S(2)}) collective-permute-start(bf16[256,640]{1,0:T(8,128)(2,1)S(1)} %copy-done.2), channel_id=1, source_target_pairs={{0,64},{64,0},{1,65},{65,1},{2,66},{66,2},{3,67},{67,3},{4,68},{68... | collective-permute-start | bytes 983048 | tf_op jit(solution)/shard_map/ppermute | solution.py:217
  24.9 28.3 %collective-permute-done.wp_ref = bf16[256,640]{1,0:T(8,128)(2,1)S(1)} collective-permute-done((bf16[256,640]{1,0:T(8,128)(2,1)S(1)}, bf16[256,640]{1,0:T(8,128)(2,1)S(1)}, u32[]{:S(2)}, u32[]{:S(2)}) %collective-permute-start) | collective-permute-done | bytes 327712 | tf_op jit(solution)/shard_map/ppermute | solution.py:217
  53.1 0.0 all-to-all-done.t_ref
  53.1 2.1 %project.1 = bf16[16,64,640]{2,1,0:T(8,128)(2,1)} custom-call(s32[1]{0:T(128)} %bitcast.1.half_ref, bf16[16,64,512]{2,1,0:T(8,128)(2,1)S(1)} %all-to-all-done.t_ref, bf16[256,640]{1,0:T(8,128)(2,1)S(1)} %copy-done.2, bf16[256,640]{1,0:T(8,128)(2,1)S(1)} %collective-permute-done.wp_ref), custom_call_target="tpu_custom_call" | custom-call | tf_op jit(solution)/shard_map/project/pallas_call | solution.py:74
  55.2 7.1 %all-to-all-start.1 = ((bf16[16,64,640]{2,1,0:T(8,128)(2,1)}), bf16[16,64,640]{2,1,0:T(8,128)(2,1)S(1)}, u32[]{:S(2)}, u32[]{:S(2)}) async-start(bf16[16,64,640]{2,1,0:T(8,128)(2,1)} %project.1), calls=%async_computation.1 | async-start | bytes 2621440 | tf_op jit(solution)/shard_map/all_to_all | solution.py:219
  62.3 0.0 copy-start.3
  62.3 1.9 %collective-permute-start.2 = (bf16[16,1,256,128]{3,2,1,0:T(8,128)(2,1)S(1)}, bf16[16,1,256,128]{3,2,1,0:T(8,128)(2,1)}, u32[]{:S(2)}, u32[]{:S(2)}) collective-permute-start(bf16[16,1,256,128]{3,2,1,0:T(8,128)(2,1)S(1)} %copy-done), channel_id=1, source_target_pairs={{0,4},{4,0},{1,5},{5,1},{2,6},{6,2},{3,7},{7,3},{8,12},{12,8},{9,1... | collective-permute-start | bytes 3145736 | tf_op jit(solution)/shard_map/ppermute | solution.py:214
  64.2 2.4 %collective-permute-start.3 = (bf16[16,1,256,128]{3,2,1,0:T(8,128)(2,1)S(1)}, bf16[16,1,256,128]{3,2,1,0:T(8,128)(2,1)}, u32[]{:S(2)}, u32[]{:S(2)}) collective-permute-start(bf16[16,1,256,128]{3,2,1,0:T(8,128)(2,1)S(1)} %copy-done.1), channel_id=1, source_target_pairs={{0,4},{4,0},{1,5},{5,1},{2,6},{6,2},{3,7},{7,3},{8,12},{12,8},{9,1... | collective-permute-start | bytes 3145736 | tf_op jit(solution)/shard_map/ppermute | solution.py:215
  66.7 0.1 add.23
  66.8 0.2 fusion
  67.0 0.1 pad_maximum_fusion
  67.1 14.6 %all-to-all-done.1.p_ref = bf16[16,64,640]{2,1,0:T(8,128)(2,1)S(1)} async-done(((bf16[16,64,640]{2,1,0:T(8,128)(2,1)}), bf16[16,64,640]{2,1,0:T(8,128)(2,1)S(1)}, u32[]{:S(2)}, u32[]{:S(2)}) %all-to-all-start.1) | async-done | bytes 1310752 | tf_op jit(solution)/shard_map/all_to_all | solution.py:219
  81.7 0.4 finish_projection.1
  82.1 1.9 %collective-permute-start.1 = (bf16[64,128]{1,0:T(8,128)(2,1)S(1)}, bf16[64,128]{1,0:T(8,128)(2,1)S(1)}, u32[]{:S(2)}, u32[]{:S(2)}) collective-permute-start(bf16[64,128]{1,0:T(8,128)(2,1)S(1)} %get-tuple-element.12.mine_ref), channel_id=1, source_target_pairs={{0,4},{4,0},{1,5},{5,1},{2,6},{6,2},{3,7},{7,3},{8,12},{12,8},{9,1... | collective-permute-start | bytes 49160 | tf_op jit(solution)/shard_map/ppermute | solution.py:232
  84.0 0.0 collective-permute-done.2.kb
  84.0 0.0 collective-permute-done.3.vb
  84.1 1.1 %collective-permute-done.1.theirs_ref = bf16[64,128]{1,0:T(8,128)(2,1)S(1)} collective-permute-done((bf16[64,128]{1,0:T(8,128)(2,1)S(1)}, bf16[64,128]{1,0:T(8,128)(2,1)S(1)}, u32[]{:S(2)}, u32[]{:S(2)}) %collective-permute-start.1) | collective-permute-done | bytes 16416 | tf_op jit(solution)/shard_map/ppermute | solution.py:232
  85.2 3.5 %attend.1 = bf16[4,64,128]{2,1,0:T(8,128)(2,1)S(1)} custom-call(s32[1]{0:T(128)} %bitcast.par_ref, s32[16]{0:T(128)S(1)} %copy-done.3, s32[16]{0:T(128)S(1)} %copy-done.4, bf16[256,128]{1,0:T(8,128)(2,1)S(1)} %get-tuple-element.11.q_ref, bf16[64,128]{1,0:T(8,128)(2,1)S(1)} %get-tuple-element.12.mine_ref, ...), custom_call_target="tpu_custom_call" | custom-call | tf_op jit(solution)/shard_map/attend/pallas_call | solution.py:192
  88.7 8.0 %all_to_all.15 = bf16[4,64,128]{2,1,0:T(8,128)(2,1)S(1)} all-to-all(bf16[4,64,128]{2,1,0:T(8,128)(2,1)S(1)} %attend.1), channel_id=1, replica_groups=mesh['x'=4,'zh'=2,'zl'=8,'core'=2,'sec'=4] {'sec'}, dimensions={0} | all-to-all | bytes 131072 | tf_op jit(solution)/shard_map/all_to_all | solution.py:246
  96.7 0.6 copy.8
  (10 shorter events, 0.0 us)
Async XLA Ops:
  2.8 7.2 %copy-start.2 = (bf16[256,640]{1,0:T(8,128)(2,1)S(1)}, bf16[256,640]{1,0:T(8,128)(2,1)}, u32[]{:S(2)}) copy-start(bf16[256,640]{1,0:T(8,128)(2,1)} %get-tuple-element.10.wo_ref) | copy-start | bytes 983044
  2.8 50.3 %all-to-all-start = ((bf16[16,64,512]{2,1,0:T(8,128)(2,1)}), bf16[16,64,512]{2,1,0:T(8,128)(2,1)S(1)}, u32[]{:S(2)}, u32[]{:S(2)}) async-start(bf16[16,64,512]{2,1,0:T(8,128)(2,1)} %get-tuple-element.9), calls=%async_computation | async-start | bytes 2097152 | tf_op jit(solution)/shard_map/all_to_all | solution.py:216
  10.0 43.1 %collective-permute-start = (bf16[256,640]{1,0:T(8,128)(2,1)S(1)}, bf16[256,640]{1,0:T(8,128)(2,1)S(1)}, u32[]{:S(2)}, u32[]{:S(2)}) collective-permute-start(bf16[256,640]{1,0:T(8,128)(2,1)S(1)} %copy-done.2), channel_id=1, source_target_pairs={{0,64},{64,0},{1,65},{65,1},{2,66},{66,2},{3,67},{67,3},{4,68},{68... | collective-permute-start | bytes 983048 | tf_op jit(solution)/shard_map/ppermute | solution.py:217
  55.2 7.1 %copy-start = (bf16[16,1,256,128]{3,2,1,0:T(8,128)(2,1)S(1)}, bf16[16,1,256,128]{3,2,1,0:T(8,128)(2,1)}, u32[]{:S(2)}) copy-start(bf16[16,1,256,128]{3,2,1,0:T(8,128)(2,1)} %ka.1) | copy-start | bytes 3145732
  55.2 9.0 %copy-start.1 = (bf16[16,1,256,128]{3,2,1,0:T(8,128)(2,1)S(1)}, bf16[16,1,256,128]{3,2,1,0:T(8,128)(2,1)}, u32[]{:S(2)}) copy-start(bf16[16,1,256,128]{3,2,1,0:T(8,128)(2,1)} %va.1) | copy-start | bytes 3145732
  55.2 11.5 %copy-start.4 = (s32[16]{0:T(128)S(1)}, s32[16]{0:T(128)}, u32[]{:S(2)}) copy-start(s32[16]{0:T(128)} %end_ref.1) | copy-start | bytes 196
  55.2 26.5 %all-to-all-start.1 = ((bf16[16,64,640]{2,1,0:T(8,128)(2,1)}), bf16[16,64,640]{2,1,0:T(8,128)(2,1)S(1)}, u32[]{:S(2)}, u32[]{:S(2)}) async-start(bf16[16,64,640]{2,1,0:T(8,128)(2,1)} %project.1), calls=%async_computation.1 | async-start | bytes 2621440 | tf_op jit(solution)/shard_map/all_to_all | solution.py:219
  62.3 22.9 %copy-start.3 = (s32[16]{0:T(128)S(1)}, s32[16]{0:T(128)}, u32[]{:S(2)}) copy-start(s32[16]{0:T(128)} %begin_ref.1) | copy-start | bytes 196
  62.3 21.7 %collective-permute-start.2 = (bf16[16,1,256,128]{3,2,1,0:T(8,128)(2,1)S(1)}, bf16[16,1,256,128]{3,2,1,0:T(8,128)(2,1)}, u32[]{:S(2)}, u32[]{:S(2)}) collective-permute-start(bf16[16,1,256,128]{3,2,1,0:T(8,128)(2,1)S(1)} %copy-done), channel_id=1, source_target_pairs={{0,4},{4,0},{1,5},{5,1},{2,6},{6,2},{3,7},{7,3},{8,12},{12,8},{9,1... | collective-permute-start | bytes 3145736 | tf_op jit(solution)/shard_map/ppermute | solution.py:214
  64.2 19.8 %collective-permute-start.3 = (bf16[16,1,256,128]{3,2,1,0:T(8,128)(2,1)S(1)}, bf16[16,1,256,128]{3,2,1,0:T(8,128)(2,1)}, u32[]{:S(2)}, u32[]{:S(2)}) collective-permute-start(bf16[16,1,256,128]{3,2,1,0:T(8,128)(2,1)S(1)} %copy-done.1), channel_id=1, source_target_pairs={{0,4},{4,0},{1,5},{5,1},{2,6},{6,2},{3,7},{7,3},{8,12},{12,8},{9,1... | collective-permute-start | bytes 3145736 | tf_op jit(solution)/shard_map/ppermute | solution.py:215
  82.1 3.1 %collective-permute-start.1 = (bf16[64,128]{1,0:T(8,128)(2,1)S(1)}, bf16[64,128]{1,0:T(8,128)(2,1)S(1)}, u32[]{:S(2)}, u32[]{:S(2)}) collective-permute-start(bf16[64,128]{1,0:T(8,128)(2,1)S(1)} %get-tuple-element.12.mine_ref), channel_id=1, source_target_pairs={{0,4},{4,0},{1,5},{5,1},{2,6},{6,2},{3,7},{7,3},{8,12},{12,8},{9,1... | collective-permute-start | bytes 49160 | tf_op jit(solution)/shard_map/ppermute | solution.py:232
